TPU v7x, 32 devices: a whole 2x2x4 slice. The times are simulated.
32 devices in a mesh: groups: 2 (over x), seq: 16 (over z, y, core).
Axes of the slice: x: 2, y: 2, z: 4, core: 2. Of those that a mesh axis runs over, the one named last changes fastest.
Arguments:
- tokens: bfloat16 [1024, 512, 512], P(('groups', 'seq')), parts along dimension 0, may hold values from -6 to 6
- cotangent: bfloat16 [1024, 512, 512], P('groups', 'seq'), parts along dimension 0, may hold values from -6 to 6
- w_first: bfloat16 [512, 512], P('seq'), may hold values from -0.25 to 0.25
- w_second: bfloat16 [512, 512], P('seq'), may hold values from -0.25 to 0.25
- mask_first: int32 [4, 4], replicated, may hold values from 0 to 1, as said below
- mask_second: int32 [4, 4], replicated, may hold values from 0 to 1, as said below
- gate_values: bfloat16 [1024, 512], P(('groups', 'seq')), parts along dimension 0, may hold values from -4 to 4
Outputs:
- grad_tokens: bfloat16 [1024, 512, 512], P(('groups', 'seq')), parts along dimension 0
- grad_first: float32 [1024, 512], P(('groups', 'seq')), parts along dimension 0
- grad_second: float32 [1024, 512], P(('groups', 'seq')), parts along dimension 0
There are 2 independent parts, one for each index of `groups`. A program takes and returns all parts, laid end to end along the dimension named above; an argument that names none is the same for every part. Nothing has to cross between parts.
Inputs may be any that keep to these rules, and one draw needn't show every extreme that they name: `mask_first`: the diagonal blocks of each factor are always kept. `mask_second`: the diagonal blocks of each factor are always kept.
All inputs are finite; a program needn't handle non-finite values.
Results may differ from a plain program's by a relative error of at most 0.0054.
Values may be sent and summed in bfloat16 or wider, within the bound.
A program may use at most 320 MiB of HBM per device.

v0:
```python
import math

import jax
import jax.numpy as jnp
from jax import lax
from jax.sharding import PartitionSpec as P

BLK = 128


def expand_rows(mask, row_ids, extent):
    labels = jnp.arange(mask.shape[0], dtype=jnp.int32)
    row_pick = ((row_ids // BLK)[:, None] == labels[None, :]).astype(jnp.float32)
    col_pick = ((jnp.arange(extent, dtype=jnp.int32) // BLK)[:, None] == labels[None, :]).astype(
        jnp.float32
    )
    return jnp.dot(jnp.dot(row_pick, mask.astype(jnp.float32)), col_pick.T)


def per_device(tokens, cotangent, w_first, w_second, mask_first, mask_second, gate_values):
    position = lax.axis_index("seq")
    extent = tokens.shape[1]
    channels = tokens.shape[2]
    shard_rows = w_first.shape[0]
    row_ids = position * shard_rows + jnp.arange(shard_rows, dtype=jnp.int32)
    keep_first = expand_rows(mask_first, row_ids, extent)
    keep_second = expand_rows(mask_second, row_ids, extent)
    local_first = (w_first.astype(jnp.float32) * keep_first).astype(jnp.bfloat16)
    local_second = (w_second.astype(jnp.float32) * keep_second).astype(jnp.bfloat16)
    full_first, full_second = (
        lax.all_gather(local_first, "seq", axis=0, tiled=True),
        lax.all_gather(local_second, "seq", axis=0, tiled=True),
    )
    gate_full = gate_values.astype(jnp.float32)[:, :, None]
    gated = tokens.astype(jnp.float32) * gate_full
    hidden = jnp.einsum("ijc,kj->ikc", tokens, full_first, preferred_element_type=jnp.float32)
    mixed = (hidden * gated).astype(jnp.bfloat16)
    columns = lax.all_to_all(mixed, "seq", split_axis=1, concat_axis=0, tiled=True)
    flat_cot = cotangent.reshape(extent, -1)
    flat_cols = columns.reshape(extent, -1)
    back_flat = lax.dot_general(
        full_second, flat_cot, (((0,), (0,)), ((), ())), preferred_element_type=jnp.float32
    )
    back_col = back_flat.astype(jnp.bfloat16).reshape(cotangent.shape)
    picked = flat_cot
    summed_second = lax.psum_scatter(
        lax.dot_general(
            picked, flat_cols, (((1,), (1,)), ((), ())), preferred_element_type=jnp.float32
        ),
        "seq",
        scatter_dimension=0,
        tiled=True,
    )
    back_rows = lax.all_to_all(back_col, "seq", split_axis=0, concat_axis=1, tiled=True)
    back_float = back_rows.astype(jnp.float32)
    back_hidden = (back_float * gated).astype(jnp.bfloat16)
    direct = gate_full * back_float * hidden
    through = jnp.einsum("ikc,kj->ijc", back_hidden, full_first, preferred_element_type=jnp.float32)
    grad_tokens = (direct + through).astype(jnp.bfloat16)
    picked = back_hidden
    summed_first = lax.psum_scatter(
        jnp.einsum("ikc,ijc->kj", picked, tokens, preferred_element_type=jnp.float32),
        "seq",
        scatter_dimension=0,
        tiled=True,
    )
    factor = 1.0 / math.sqrt(extent * channels)
    grad_first = keep_first * summed_first * factor
    grad_second = keep_second * summed_second * factor
    return (grad_tokens, grad_first, grad_second)


def solution(mesh):
    in_specs = (
        P(("groups", "seq"), None, None),
        P("groups", "seq", None),
        P("seq", None),
        P("seq", None),
        P(),
        P(),
        P(("groups", "seq"), None),
    )
    out_specs = (
        P(("groups", "seq"), None, None),
        P(("groups", "seq"), None),
        P(("groups", "seq"), None),
    )
    return jax.shard_map(
        per_device, mesh=mesh, in_specs=in_specs, out_specs=out_specs, check_vma=False
    )
```

profile of v0, /device:TPU:0, one launch (start us, length us, event | category | flops | bytes accessed | tf_op | source)
XLA Modules:
  0.0 1033.5 jit_solution(2067010824254078379)
XLA Ops:
  7.2 1.8 multiply_convert_fusion.1
  9.0 24.6 %all_gather.6 = bf16[512,512]{1,0:T(8,128)(2,1)S(1)} all-gather(bf16[32,512]{1,0:T(8,128)(2,1)S(1)} %get-tuple-element.5), channel_id=1, replica_groups=mesh['groups'=2,'seq'=16] {'seq'}, dimensions={0}, use_global_device_ids=true | all-gather | bytes 557056 | tf_op jit(solution)/shard_map/all_gather | solution.py:32
  33.6 18.4 %copy.20 = bf16[64,8,32,512]{3,1,2,0:T(8,128)(2,1)} copy(bf16[64,8,32,512]{3,2,1,0:T(8,128)(2,1)} %bitcast.55) | data formatting | bytes 33554432
  52.0 18.1 %convolution_convert_fusion = bf16[512,16384]{1,0:T(8,128)(2,1)} fusion(bf16[512,512]{1,0:T(8,128)(2,1)S(1)} %all_gather.6, bf16[512,16384]{1,0:T(8,128)(2,1)} %bitcast.50), kind=kOutput, calls=%fused_computation.9 | convolution fusion | flops 8598323200 | bytes 34078720 | tf_op jit(solution)/shard_map/dot_general | solution.py:41
  70.1 16.6 %copy.21 = bf16[64,8,32,512]{3,2,1,0:T(8,128)(2,1)} copy(bf16[64,8,32,512]{3,1,2,0:T(8,128)(2,1)} %bitcast.52) | data formatting | bytes 33554432
  86.7 0.0 copy-start.2
  86.7 0.0 copy-start.3
  86.7 0.0 copy-start.4
  86.7 5.3 all-to-all-start
  92.0 0.0 copy-done.2
  92.0 0.0 copy-done.3
  92.0 0.0 copy-done.4
  92.1 1.0 multiply_convert_fusion
  93.1 323.6 %all_gather.7 = bf16[512,512]{1,0:T(8,128)(2,1)S(1)} all-gather(bf16[32,512]{1,0:T(8,128)(2,1)S(1)} %get-tuple-element.7), channel_id=1, replica_groups=mesh['groups'=2,'seq'=16] {'seq'}, dimensions={0}, use_global_device_ids=true | all-gather | bytes 557056 | tf_op jit(solution)/shard_map/all_gather | solution.py:31
  416.6 0.0 all-to-all-done
  416.6 18.8 %copy.15 = f32[16,32,32,512]{3,2,0,1:T(8,128)} copy(bf16[16,32,32,512]{3,2,1,0:T(8,128)(2,1)} %bitcast.11) | data formatting | bytes 50331648 | tf_op jit(solution)/shard_map/convert_element_type | solution.py:55
  435.5 44.3 %fusion.3 = (bf16[32,512,512]{2,1,0:T(8,128)(2,1)}, bf16[32,512,512]{2,1,0:T(8,128)(2,1)}, f32[512,32,512]{2,0,1:T(8,128)}) fusion(bf16[32,512,512]{2,1,0:T(8,128)(2,1)} %param.7, f32[32,512]{1,0:T(8,128)S(1)} %convert_element_type.52, f32[16,32,32,512]{3,2,0,1:T(8,128)} %copy.15, bf16[512,512]{1,0:T(8,128)(2,1)S(1)} %all_gather.7), kind=kOutput, calls=%fused_computation.7 | convolution fusion | flops 8640266240 | bytes 118030336 | tf_op jit(solution)/shard_map/ijc,kj->ikc/dot_general | solution.py:36
  479.8 18.4 %copy.16 = bf16[32,512,512]{2,0,1:T(8,128)(2,1)} copy(bf16[32,512,512]{2,1,0:T(8,128)(2,1)} %get-tuple-element.3) | data formatting | bytes 33554432 | tf_op jit(solution)/shard_map/convert_element_type | solution.py:37
  498.3 53.5 %all-to-all-start.1 = ((bf16[32,512,512]{2,0,1:T(8,128)(2,1)}), bf16[32,512,512]{2,0,1:T(8,128)(2,1)}, u32[]{:S(2)}, u32[]{:S(2)}) async-start(bf16[32,512,512]{2,0,1:T(8,128)(2,1)} %copy.16), calls=%async_computation.2 | async-start | bytes 33554432 | tf_op jit(solution)/shard_map/all_to_all | solution.py:38
  551.8 0.0 reduce-scatter.3.cloned.1.call-start
  551.8 18.1 %convolution_bitcast_fusion.1 = f32[512,512]{1,0:T(8,128)} fusion(bf16[32,512,512]{2,1,0:T(8,128)(2,1)} %get-tuple-element.4, bf16[32,512,512]{2,1,0:T(8,128)(2,1)} %param.7), kind=kOutput, calls=%fused_computation.11 | convolution fusion | flops 8589934592 | bytes 34603008 | tf_op jit(solution)/shard_map/ikc,ijc->kj/dot_general | solution.py:62
  569.9 0.0 reduce-scatter.3.cloned.1.call-update
  569.9 0.3 reduce-scatter.5.cloned.1.call-start
  570.2 285.0 %all-to-all-done.1 = bf16[32,512,512]{2,0,1:T(8,128)(2,1)} async-done(((bf16[32,512,512]{2,0,1:T(8,128)(2,1)}), bf16[32,512,512]{2,0,1:T(8,128)(2,1)}, u32[]{:S(2)}, u32[]{:S(2)}) %all-to-all-start.1) | async-done | bytes 16777248 | tf_op jit(solution)/shard_map/all_to_all | solution.py:38
  855.2 15.8 %copy.17 = bf16[32,16,32,512]{3,2,0,1:T(8,128)(2,1)S(1)} copy(bf16[32,16,32,512]{3,0,2,1:T(8,128)(2,1)} %bitcast.8) | data formatting | bytes 33554432 | tf_op jit(solution)/shard_map/all_to_all | solution.py:38
  871.0 12.2 %copy.22 = bf16[64,8,32,512]{3,1,2,0:T(8,128)(2,1)} copy(bf16[64,8,32,512]{3,2,1,0:T(8,128)(2,1)S(1)} %bitcast.54) | data formatting | bytes 33554432
  883.2 18.1 %convolution_bitcast_fusion = f32[512,512]{1,0:T(8,128)} fusion(bf16[512,16384]{1,0:T(8,128)(2,1)} %bitcast.56, bf16[512,16384]{1,0:T(8,128)(2,1)} %bitcast.51), kind=kOutput, calls=%fused_computation.10 | convolution fusion | flops 8589934592 | bytes 34603008 | tf_op jit(solution)/shard_map/dot_general | solution.py:47
  901.3 0.0 reduce-scatter.5.cloned.1.call-update
  901.3 0.0 copy-start.1
  901.3 0.0 copy-start
  901.3 34.4 %fusion = bf16[32,512,512]{2,1,0:T(8,128)(2,1)} fusion(f32[16,32,32,512]{3,2,0,1:T(8,128)} %copy.15, f32[512,32,512]{2,0,1:T(8,128)} %get-tuple-element.9, f32[32,512]{1,0:T(8,128)S(1)} %convert_element_type.52, bf16[32,512,512]{2,1,0:T(8,128)(2,1)} %get-tuple-element.4, bf16[512,512]{1,0:T(8,128)(2,1)S(1)} %all_gather.7), kind=kOutput, calls=%fused_computation.1 | convolution fusion | flops 8623489024 | bytes 101253120 | tf_op jit(solution)/shard_map/ikc,kj->ijc/dot_general | solution.py:58
  935.7 0.0 reduce-scatter.3.cloned.1.call-done
  935.7 0.0 copy-done.1
  935.7 1.5 multiply_multiply_fusion.1
  937.2 88.0 %reduce-scatter.5.cloned.1.call-done = f32[32,512]{1,0:T(8,128)} async-done(((f32[512,512]{1,0:T(8,128)}), f32[32,512]{1,0:T(8,128)}) %reduce-scatter.5.cloned.1.call-update) | async-done | bytes 65552 | tf_op jit(solution)/shard_map/reduce_scatter | solution.py:46
  1025.2 0.0 copy-done
  1025.2 1.5 multiply_multiply_fusion
  (3 shorter events, 0.0 us)
Async XLA Ops:
  86.7 5.3 copy-start.2
  86.7 5.4 copy-start.3
  86.7 5.4 copy-start.4
  86.7 330.0 %all-to-all-start = ((bf16[512,32,512]{2,1,0:T(8,128)(2,1)}), bf16[512,32,512]{2,1,0:T(8,128)(2,1)}, u32[]{:S(2)}, u32[]{:S(2)}) async-start(bf16[512,32,512]{2,1,0:T(8,128)(2,1)} %bitcast.53), calls=%async_computation | async-start | bytes 33554432 | tf_op jit(solution)/shard_map/all_to_all | solution.py:54
  498.3 356.9 %all-to-all-start.1 = ((bf16[32,512,512]{2,0,1:T(8,128)(2,1)}), bf16[32,512,512]{2,0,1:T(8,128)(2,1)}, u32[]{:S(2)}, u32[]{:S(2)}) async-start(bf16[32,512,512]{2,0,1:T(8,128)(2,1)} %copy.16), calls=%async_computation.2 | async-start | bytes 33554432 | tf_op jit(solution)/shard_map/all_to_all | solution.py:38
  551.8 384.0 %reduce-scatter.3.cloned.1.call-start = ((), (), s32[]{:S(2)}) async-start(), calls=%async_computation.4 | async-start | bytes 1114112 | tf_op jit(solution)/shard_map/reduce_scatter | solution.py:61
  569.9 455.2 %reduce-scatter.5.cloned.1.call-start = ((), (), s32[]{:S(2)}) async-start(), calls=%async_computation.5 | async-start | bytes 1114112 | tf_op jit(solution)/shard_map/reduce_scatter | solution.py:46
  901.3 34.4 %copy-start.1 = (f32[32,512]{1,0:T(8,128)S(1)}, f32[32,512]{1,0:T(8,128)}, u32[]{:S(2)}) copy-start(f32[32,512]{1,0:T(8,128)} %get-tuple-element.8) | copy-start | bytes 196612
  901.3 123.9 %copy-start = (f32[32,512]{1,0:T(8,128)S(1)}, f32[32,512]{1,0:T(8,128)}, u32[]{:S(2)}) copy-start(f32[32,512]{1,0:T(8,128)} %get-tuple-element.6) | copy-start | bytes 196612
Sparse Core Ops, SparseCore 0:
  570.1 264.4 reduce-scatter.2
  901.4 123.7 reduce-scatter.4
where the time goes:
time: 1030 us
  waiting for transfers between devices  373 us (36%)
  blocking collectives  348 us (34%)
  matrix products  136 us (13%)
  local copies, waits for them, and re-layouts  100 us (10%)
  starting transfers between devices  59.1 us (6%)
  between operations  14.1 us (1%)
    all_gather x1, blocking collectives, per_device(): lax.all_gather(local_first, 'seq', axis=0, tiled=True)  324 us
    all_to_all x1, waiting for transfers between devices, per_device(): lax.all_to_all(mixed, 'seq', split_axis=1, concat_axis=0, tiled=True)  285 us
    reduce_scatter x1, waiting for transfers between devices, per_device(): lax.psum_scatter(lax.dot_general(picked, flat_cols, (((1,), (1,)), ((), (...  88 us
    all_to_all x1, starting transfers between devices, per_device(): lax.all_to_all(mixed, 'seq', split_axis=1, concat_axis=0, tiled=True)  53.5 us
    unnamed x13, local copies, waits for them, and re-layouts  47.2 us
    dot_general x1, matrix products, per_device(): jnp.einsum('ijc,kj->ikc', tokens, full_first, preferred_element_type=jnp....  44.3 us
    dot_general x1, matrix products, per_device(): jnp.einsum('ikc,kj->ijc', back_hidden, full_first, preferred_element_type...  34.4 us
    all_gather x1, blocking collectives, per_device(): lax.all_gather(local_second, 'seq', axis=0, tiled=True)  24.6 us
  transfers between devices with their start and end apart: 4, of which 2 were waited for; matrix products, arithmetic and copies ran while one was open for 10% of the time, Pallas kernels for 0%

commit v1 on v0

--- a/solution.py
+++ b/solution.py
@@ -27,43 +27,41 @@
     keep_second = expand_rows(mask_second, row_ids, extent)
     local_first = (w_first.astype(jnp.float32) * keep_first).astype(jnp.bfloat16)
     local_second = (w_second.astype(jnp.float32) * keep_second).astype(jnp.bfloat16)
-    full_first, full_second = (
-        lax.all_gather(local_first, "seq", axis=0, tiled=True),
-        lax.all_gather(local_second, "seq", axis=0, tiled=True),
-    )
-    gate_full = gate_values.astype(jnp.float32)[:, :, None]
-    gated = tokens.astype(jnp.float32) * gate_full
-    hidden = jnp.einsum("ijc,kj->ikc", tokens, full_first, preferred_element_type=jnp.float32)
-    mixed = (hidden * gated).astype(jnp.bfloat16)
-    columns = lax.all_to_all(mixed, "seq", split_axis=1, concat_axis=0, tiled=True)
+    full = lax.all_gather(jnp.stack([local_first, local_second]), "seq", axis=1, tiled=True)
+    full_first, full_second = full[0], full[1]
+    shards = extent // shard_rows
     flat_cot = cotangent.reshape(extent, -1)
-    flat_cols = columns.reshape(extent, -1)
     back_flat = lax.dot_general(
         full_second, flat_cot, (((0,), (0,)), ((), ())), preferred_element_type=jnp.float32
     )
     back_col = back_flat.astype(jnp.bfloat16).reshape(cotangent.shape)
-    picked = flat_cot
-    summed_second = lax.psum_scatter(
-        lax.dot_general(
-            picked, flat_cols, (((1,), (1,)), ((), ())), preferred_element_type=jnp.float32
-        ),
-        "seq",
-        scatter_dimension=0,
-        tiled=True,
-    )
     back_rows = lax.all_to_all(back_col, "seq", split_axis=0, concat_axis=1, tiled=True)
+    tokens_late, back_col = lax.optimization_barrier((tokens, back_col))
+    gate_full = gate_values.astype(jnp.float32)[:, :, None]
+    gated = tokens_late.astype(jnp.float32) * gate_full
+    hidden = jnp.einsum("ijc,kj->ikc", tokens_late, full_first, preferred_element_type=jnp.float32)
+    mixed = (hidden * gated).astype(jnp.bfloat16)
+    mixed, back_rows = lax.optimization_barrier((mixed, back_rows))
+    columns = lax.all_to_all(mixed, "seq", split_axis=1, concat_axis=0, tiled=True)
+    flat_cols = columns.reshape(extent, -1)
     back_float = back_rows.astype(jnp.float32)
     back_hidden = (back_float * gated).astype(jnp.bfloat16)
     direct = gate_full * back_float * hidden
     through = jnp.einsum("ikc,kj->ijc", back_hidden, full_first, preferred_element_type=jnp.float32)
     grad_tokens = (direct + through).astype(jnp.bfloat16)
-    picked = back_hidden
     summed_first = lax.psum_scatter(
-        jnp.einsum("ikc,ijc->kj", picked, tokens, preferred_element_type=jnp.float32),
+        jnp.einsum("ikc,ijc->kj", back_hidden, tokens_late, preferred_element_type=jnp.float32),
         "seq",
         scatter_dimension=0,
         tiled=True,
     )
+    part_second = lax.dot_general(
+        flat_cot, flat_cols, (((1,), (1,)), ((), ())), preferred_element_type=jnp.float32
+    )
+    spread = lax.all_to_all(
+        part_second.reshape(shards, shard_rows, extent), "seq", split_axis=0, concat_axis=0, tiled=True
+    )
+    summed_second = jnp.sum(spread, axis=0)
     factor = 1.0 / math.sqrt(extent * channels)
     grad_first = keep_first * summed_first * factor
     grad_second = keep_second * summed_second * factor

time: 1030 us -> 965 us (0.937)
  blocking collectives: 348 us -> 0 us
  waiting for transfers between devices: 373 us -> 569 us
  starting transfers between devices: 59.1 us -> 146 us
  matrix products: 136 us -> 124 us
    all_gather x2 -> x0, blocking collectives: 348 us -> none  [the longest x1 324 us: per_device(): lax.all_gather(local_first, 'seq', axis=0, tiled=True)]
    all_to_all x1, waiting for transfers between devices: 0.01 us -> 268 us  [per_device(): lax.all_to_all(back_col, 'seq', split_axis=0, concat_axis=1, tiled=True)]
    reduce_scatter x2 -> x1, waiting for transfers between devices: 88 us -> 0.01 us  [per_device(): lax.psum_scatter(jnp.einsum('ikc,ijc->kj', back_hidden, tokens_late, pref...]
    all_to_all x0 -> x1, starting transfers between devices: none -> 70.2 us  [per_device(): lax.all_to_all(part_second.reshape(shards, shard_rows, extent), 'seq', sp...]
    convert_element_type x2 -> x0, local copies, waits for them, and re-layouts: 37.3 us -> none  [the longest x1 18.8 us: per_device(): back_float = back_rows.astype(jnp.float32)]
    optimization_barrier x0 -> x1, local copies, waits for them, and re-layouts: none -> 26.5 us  [per_device(): mixed, back_rows = lax.optimization_barrier((mixed, back_rows))]
    all_gather x0 -> x1, waiting for transfers between devices: none -> 22.4 us  [per_device(): lax.all_gather(jnp.stack([local_first, local_second]), 'seq', axis=1, til...]
    all_to_all x1, starting transfers between devices: 53.5 us -> 70.2 us  [per_device(): lax.all_to_all(mixed, 'seq', split_axis=1, concat_axis=0, tiled=True)]
  transfers between devices with their start and end apart: 4 -> 5, of which waited for: 2 -> 3; matrix products, arithmetic and copies ran while one was open for 10% -> 16% of each run, Pallas kernels for 0% -> 0%
where the time goes in v1:
time: 965 us; the launch traced here: 964 us
  waiting for transfers between devices  569 us (59%)
  starting transfers between devices  146 us (15%)
  matrix products  124 us (13%)
  local copies, waits for them, and re-layouts  106 us (11%)
  between operations  14.2 us (1%)
    all_to_all x1, waiting for transfers between devices, per_device(): lax.all_to_all(mixed, 'seq', split_axis=1, concat_axis=0, tiled=True)  279 us
    all_to_all x1, waiting for transfers between devices, per_device(): lax.all_to_all(back_col, 'seq', split_axis=0, concat_axis=1, tiled=True)  268 us
    all_to_all x1, starting transfers between devices, per_device(): lax.all_to_all(part_second.reshape(shards, shard_rows, extent), 'seq', sp...  70.2 us
    all_to_all x1, starting transfers between devices, per_device(): lax.all_to_all(mixed, 'seq', split_axis=1, concat_axis=0, tiled=True)  70.2 us
    unnamed x17, local copies, waits for them, and re-layouts  49 us
    dot_general x1, matrix products, per_device(): jnp.einsum('ikc,kj->ijc', back_hidden, full_first, preferred_element_type...  36.2 us
    dot_general x1, matrix products, per_device(): jnp.einsum('ijc,kj->ikc', tokens_late, full_first, preferred_element_type...  28.2 us
    optimization_barrier x1, local copies, waits for them, and re-layouts, per_device(): mixed, back_rows = lax.optimization_barrier((mixed, back_rows))  26.5 us
  transfers between devices with their start and end apart: 5, of which 3 were waited for; matrix products, arithmetic and copies ran while one was open for 16% of the time, Pallas kernels for 0%

profile of v1, /device:TPU:0, one launch (start us, length us, event | category | flops | bytes accessed | tf_op | source)
XLA Modules:
  0.0 964.3 jit_solution(4726643977585891241)
XLA Ops:
  7.2 0.0 all-gather.2.cloned.1.call-start
  7.2 1.1 fusion.14
  8.3 0.0 copy-start.2
  8.3 1.1 fusion.17
  9.4 0.0 copy-start.4
  9.4 0.8 fusion.23
  10.2 0.6 pad_maximum_fusion
  10.9 0.0 all-gather.2.cloned.1.call-update
  10.9 18.5 %copy.21 = bf16[64,8,32,512]{3,1,2,0:T(8,128)(2,1)} copy(bf16[64,8,32,512]{3,2,1,0:T(8,128)(2,1)} %bitcast.58) | data formatting | bytes 33554432
  29.3 0.0 copy-done.2
  29.3 0.0 copy-done.4
  29.3 22.4 %all-gather.2.cloned.1.call-done = bf16[2,512,512]{2,1,0:T(8,128)(2,1)} async-done(((bf16[2,32,512]{2,1,0:T(8,128)(2,1)}), bf16[2,512,512]{2,1,0:T(8,128)(2,1)}) %all-gather.2.cloned.1.call-update) | async-done | bytes 1048592 | tf_op jit(solution)/shard_map/all_gather | solution.py:30
  51.7 15.8 %convolution_convert_fusion = bf16[512,16384]{1,0:T(8,128)(2,1)} fusion(bf16[512,16384]{1,0:T(8,128)(2,1)} %bitcast.53, bf16[2,512,512]{2,1,0:T(8,128)(2,1)} %all-gather.2.cloned.1.call-done), kind=kOutput, calls=%fused_computation.9 | convolution fusion | flops 8598323200 | bytes 34078720 | tf_op jit(solution)/shard_map/dot_general | solution.py:34
  67.5 16.6 %copy.22 = bf16[64,8,32,512]{3,2,1,0:T(8,128)(2,1)} copy(bf16[64,8,32,512]{3,1,2,0:T(8,128)(2,1)} %bitcast.55) | data formatting | bytes 33554432
  84.0 0.0 copy-start.6
  84.0 0.0 copy-start.1
  84.0 5.5 all-to-all-start
  89.5 0.0 copy-done.6
  89.5 0.0 copy-done.1
  89.6 28.2 %fusion.4 = (bf16[32,512,512]{2,1,0:T(8,128)(2,1)}, f32[512,32,512]{2,0,1:T(8,128)}) fusion(bf16[32,512,512]{2,1,0:T(8,128)(2,1)} %param.7, f32[32,512]{1,0:T(8,128)S(1)} %convert_element_type.43, bf16[2,512,512]{2,1,0:T(8,128)(2,1)S(1)} %copy-done.1), kind=kOutput, calls=%fused_computation.7 | convolution fusion | flops 8623489024 | bytes 84475904 | tf_op jit(solution)/shard_map/ijc,kj->ikc/dot_general | solution.py:42
  117.7 268.3 %all-to-all-done = bf16[512,32,512]{2,1,0:T(8,128)(2,1)} async-done(((bf16[512,32,512]{2,1,0:T(8,128)(2,1)}), bf16[512,32,512]{2,1,0:T(8,128)(2,1)}, u32[]{:S(2)}, u32[]{:S(2)}) %all-to-all-start) | async-done | bytes 16777248 | tf_op jit(solution)/shard_map/all_to_all | solution.py:38
  386.0 0.0 copy-start
  386.0 15.1 %copy.15 = bf16[16,32,32,512]{3,2,0,1:T(8,128)(2,1)} copy(bf16[16,32,32,512]{3,2,1,0:T(8,128)(2,1)} %bitcast.6) | data formatting | bytes 33554432 | tf_op jit(solution)/shard_map/all_to_all | solution.py:38
  401.1 1.8 copy-done
  402.9 26.5 %copy.17 = bf16[32,512,512]{2,0,1:T(8,128)(2,1)} copy(bf16[32,512,512]{2,1,0:T(8,128)(2,1)S(1)} %copy-done) | data formatting | bytes 33554432 | tf_op jit(solution)/shard_map/optimization_barrier | solution.py:44
  429.4 70.2 %all-to-all-start.1 = ((bf16[32,512,512]{2,0,1:T(8,128)(2,1)}), bf16[32,512,512]{2,0,1:T(8,128)(2,1)}, u32[]{:S(2)}, u32[]{:S(2)}) async-start(bf16[32,512,512]{2,0,1:T(8,128)(2,1)} %copy.17), calls=%async_computation.2 | async-start | bytes 33554432 | tf_op jit(solution)/shard_map/all_to_all | solution.py:45
  499.7 0.3 reduce-scatter.2.cloned.1.call-start
  499.9 24.1 %fusion.11 = f32[512,512]{1,0:T(8,128)} fusion(bf16[32,512,512]{2,1,0:T(8,128)(2,1)} %param.7, bf16[32,512,512]{2,1,0:T(8,128)(2,1)} %bitcast.59, f32[32,512]{1,0:T(8,128)S(1)} %convert_element_type.43), kind=kOutput, calls=%fused_computation.12 | convolution fusion | flops 8631877632 | bytes 34668544 | tf_op jit(solution)/shard_map/ikc,ijc->kj/dot_general | solution.py:53
  524.0 0.0 reduce-scatter.2.cloned.1.call-update
  524.1 278.7 %all-to-all-done.1 = bf16[32,512,512]{2,0,1:T(8,128)(2,1)} async-done(((bf16[32,512,512]{2,0,1:T(8,128)(2,1)}), bf16[32,512,512]{2,0,1:T(8,128)(2,1)}, u32[]{:S(2)}, u32[]{:S(2)}) %all-to-all-start.1) | async-done | bytes 16777248 | tf_op jit(solution)/shard_map/all_to_all | solution.py:45
  802.8 15.8 %copy.18 = bf16[32,16,32,512]{3,2,0,1:T(8,128)(2,1)S(1)} copy(bf16[32,16,32,512]{3,0,2,1:T(8,128)(2,1)} %bitcast.12) | data formatting | bytes 33554432 | tf_op jit(solution)/shard_map/all_to_all | solution.py:45
  818.6 12.2 %copy.23 = bf16[64,8,32,512]{3,1,2,0:T(8,128)(2,1)} copy(bf16[64,8,32,512]{3,2,1,0:T(8,128)(2,1)S(1)} %bitcast.57) | data formatting | bytes 33554432
  830.8 18.0 %fusion.36 = f32[512,512]{0,1:T(8,128)} fusion(bf16[512,16384]{1,0:T(8,128)(2,1)} %bitcast.61, bf16[512,16384]{1,0:T(8,128)(2,1)} %bitcast.54), kind=kOutput, calls=%fused_computation.46 | convolution fusion | flops 8589934592 | bytes 34603008 | tf_op jit(solution)/shard_map/dot_general | solution.py:58
  848.9 70.2 %all-to-all-start.2 = ((f32[16,32,512]{2,1,0:T(8,128)}), f32[16,32,512]{2,1,0:T(8,128)S(1)}, u32[]{:S(2)}, u32[]{:S(2)}) async-start(f32[16,32,512]{2,1,0:T(8,128)} %bitcast.15), calls=%async_computation.3 | async-start | bytes 2097152 | tf_op jit(solution)/shard_map/all_to_all | solution.py:61
  919.1 0.0 copy-start.5
  919.1 0.0 copy-start.3
  919.1 36.2 %fusion.2 = bf16[32,512,512]{2,1,0:T(8,128)(2,1)} fusion(bf16[32,512,512]{2,1,0:T(8,128)(2,1)} %bitcast.60, f32[512,32,512]{2,0,1:T(8,128)} %get-tuple-element.10, f32[32,512]{1,0:T(8,128)S(1)} %convert_element_type.43, bf16[32,512,512]{2,1,0:T(8,128)(2,1)} %param.7, bf16[2,512,512]{2,1,0:T(8,128)(2,1)S(1)} %copy-done.1), kind=kOutput, calls=%fused_computation.4 | convolution fusion | flops 8673820672 | bytes 101318656 | tf_op jit(solution)/shard_map/ikc,kj->ijc/dot_general | solution.py:50
  955.3 0.0 reduce-scatter.2.cloned.1.call-done
  955.3 0.0 copy-done.5
  955.3 1.5 multiply_multiply_fusion.1
  956.8 0.0 all-to-all-done.2
  956.8 0.1 reduce_sum.9
  956.9 0.0 copy-done.3
  956.9 0.6 multiply_multiply_fusion
  (3 shorter events, 0.0 us)
Async XLA Ops:
  7.2 44.5 %all-gather.2.cloned.1.call-start = ((), (), s32[]{:S(2)}) async-start(), calls=%async_computation.4 | async-start | bytes 1114112 | tf_op jit(solution)/shard_map/all_gather | solution.py:30
  8.3 21.0 %copy-start.2 = (f32[32,512]{1,0:T(8,128)}, f32[32,512]{1,0:T(8,128)S(1)}, u32[]{:S(2)}) copy-start(f32[32,512]{1,0:T(8,128)S(1)} %fusion.14) | copy-start | bytes 196612
  9.4 19.9 %copy-start.4 = (f32[32,512]{1,0:T(8,128)}, f32[32,512]{1,0:T(8,128)S(1)}, u32[]{:S(2)}) copy-start(f32[32,512]{1,0:T(8,128)S(1)} %fusion.17) | copy-start | bytes 196612
  84.0 5.5 copy-start.6
  84.0 5.5 copy-start.1
  84.0 302.0 %all-to-all-start = ((bf16[512,32,512]{2,1,0:T(8,128)(2,1)}), bf16[512,32,512]{2,1,0:T(8,128)(2,1)}, u32[]{:S(2)}, u32[]{:S(2)}) async-start(bf16[512,32,512]{2,1,0:T(8,128)(2,1)} %bitcast.56), calls=%async_computation | async-start | bytes 33554432 | tf_op jit(solution)/shard_map/all_to_all | solution.py:38
  386.0 16.9 %copy-start = (bf16[32,512,512]{2,1,0:T(8,128)(2,1)S(1)}, bf16[32,512,512]{2,1,0:T(8,128)(2,1)}, u32[]{:S(2)}) copy-start(bf16[32,512,512]{2,1,0:T(8,128)(2,1)} %get-tuple-element.8) | copy-start | bytes 50331652
  429.4 373.4 %all-to-all-start.1 = ((bf16[32,512,512]{2,0,1:T(8,128)(2,1)}), bf16[32,512,512]{2,0,1:T(8,128)(2,1)}, u32[]{:S(2)}, u32[]{:S(2)}) async-start(bf16[32,512,512]{2,0,1:T(8,128)(2,1)} %copy.17), calls=%async_computation.2 | async-start | bytes 33554432 | tf_op jit(solution)/shard_map/all_to_all | solution.py:45
  499.7 455.6 %reduce-scatter.2.cloned.1.call-start = ((), (), s32[]{:S(2)}) async-start(), calls=%async_computation.5 | async-start | bytes 1114112 | tf_op jit(solution)/shard_map/reduce_scatter | solution.py:52
  848.9 107.9 %all-to-all-start.2 = ((f32[16,32,512]{2,1,0:T(8,128)}), f32[16,32,512]{2,1,0:T(8,128)S(1)}, u32[]{:S(2)}, u32[]{:S(2)}) async-start(f32[16,32,512]{2,1,0:T(8,128)} %bitcast.15), calls=%async_computation.3 | async-start | bytes 2097152 | tf_op jit(solution)/shard_map/all_to_all | solution.py:61
  919.1 36.2 %copy-start.5 = (f32[32,512]{1,0:T(8,128)S(1)}, f32[32,512]{1,0:T(8,128)}, u32[]{:S(2)}) copy-start(f32[32,512]{1,0:T(8,128)} %copy-done.4) | copy-start | bytes 196612
  919.1 37.7 %copy-start.3 = (f32[32,512]{1,0:T(8,128)S(1)}, f32[32,512]{1,0:T(8,128)}, u32[]{:S(2)}) copy-start(f32[32,512]{1,0:T(8,128)} %copy-done.2) | copy-start | bytes 196612
Sparse Core Ops, SparseCore 0:
  11.0 40.6 all-gather.1
  524.2 257.9 reduce-scatter.1

commit v2 on v1

--- a/solution.py
+++ b/solution.py
@@ -30,33 +30,42 @@
     full = lax.all_gather(jnp.stack([local_first, local_second]), "seq", axis=1, tiled=True)
     full_first, full_second = full[0], full[1]
     shards = extent // shard_rows
-    flat_cot = cotangent.reshape(extent, -1)
+    rows = tokens.shape[0]
+    cols = cotangent.shape[1]
+    flat_cot = lax.optimization_barrier(cotangent.reshape(extent, cols * channels))
     back_flat = lax.dot_general(
         full_second, flat_cot, (((0,), (0,)), ((), ())), preferred_element_type=jnp.float32
-    )
-    back_col = back_flat.astype(jnp.bfloat16).reshape(cotangent.shape)
-    back_rows = lax.all_to_all(back_col, "seq", split_axis=0, concat_axis=1, tiled=True)
-    tokens_late, back_col = lax.optimization_barrier((tokens, back_col))
+    ).astype(jnp.bfloat16)
+    back_send = lax.optimization_barrier(back_flat.reshape(shards, rows, cols * channels))
+    back_recv = lax.all_to_all(back_send, "seq", split_axis=0, concat_axis=0, tiled=True)
+    tokens_late, back_send = lax.optimization_barrier((tokens, back_send))
     gate_full = gate_values.astype(jnp.float32)[:, :, None]
     gated = tokens_late.astype(jnp.float32) * gate_full
     hidden = jnp.einsum("ijc,kj->ikc", tokens_late, full_first, preferred_element_type=jnp.float32)
     mixed = (hidden * gated).astype(jnp.bfloat16)
-    mixed, back_rows = lax.optimization_barrier((mixed, back_rows))
-    columns = lax.all_to_all(mixed, "seq", split_axis=1, concat_axis=0, tiled=True)
-    flat_cols = columns.reshape(extent, -1)
+    mixed_send = mixed.reshape(rows, shards, cols * channels).transpose(1, 0, 2)
+    mixed_send, back_recv = lax.optimization_barrier((mixed_send, back_recv))
+    flat_cols = lax.all_to_all(mixed_send, "seq", split_axis=0, concat_axis=0, tiled=True)
+    back_rows = (
+        back_recv.reshape(shards, rows, cols, channels).transpose(1, 0, 2, 3).reshape(tokens.shape)
+    )
     back_float = back_rows.astype(jnp.float32)
     back_hidden = (back_float * gated).astype(jnp.bfloat16)
     direct = gate_full * back_float * hidden
     through = jnp.einsum("ikc,kj->ijc", back_hidden, full_first, preferred_element_type=jnp.float32)
     grad_tokens = (direct + through).astype(jnp.bfloat16)
-    summed_first = lax.psum_scatter(
-        jnp.einsum("ikc,ijc->kj", back_hidden, tokens_late, preferred_element_type=jnp.float32),
-        "seq",
-        scatter_dimension=0,
-        tiled=True,
+    part_first = jnp.einsum(
+        "ikc,ijc->kj", back_hidden, tokens_late, preferred_element_type=jnp.float32
+    )
+    summed_first = lax.psum_scatter(part_first, "seq", scatter_dimension=0, tiled=True)
+    flat_cols, grad_tokens, part_first = lax.optimization_barrier(
+        (flat_cols, grad_tokens, part_first)
     )
     part_second = lax.dot_general(
-        flat_cot, flat_cols, (((1,), (1,)), ((), ())), preferred_element_type=jnp.float32
+        flat_cot,
+        flat_cols.reshape(extent, cols * channels),
+        (((1,), (1,)), ((), ())),
+        preferred_element_type=jnp.float32,
     )
     spread = lax.all_to_all(
         part_second.reshape(shards, shard_rows, extent), "seq", split_axis=0, concat_axis=0, tiled=True

time: 965 us -> 899 us (0.932)
  waiting for transfers between devices: 569 us -> 508 us
  other arithmetic: 3.67 us -> 25.8 us
  local copies, waits for them, and re-layouts: 106 us -> 86.6 us
    all_to_all x2, waiting for transfers between devices: 547 us -> 423 us  [the longest x1 224 us: per_device(): lax.all_to_all(back_send, 'seq', split_axis=0, concat_axis=0, tiled=True)]
    reduce_scatter x1, waiting for transfers between devices: 0.01 us -> 62.5 us  [per_device(): lax.psum_scatter(part_first, 'seq', scatter_dimension=0, tiled=True)]
    reshape x0 -> x2, local copies, waits for them, and re-layouts: none -> 44.2 us  [per_device(): mixed_send = mixed.reshape(rows, shards, cols * channels).transpose(1, 0, 2)]
    all_to_all x2 -> x0, local copies, waits for them, and re-layouts: 30.9 us -> none  [the longest x1 15.8 us: per_device(): lax.all_to_all(mixed, 'seq', split_axis=1, concat_axis=0, tiled=True)]
    optimization_barrier x1 -> x0, local copies, waits for them, and re-layouts: 26.5 us -> none  [per_device(): mixed, back_rows = lax.optimization_barrier((mixed, back_rows))]
    convert_element_type x0 -> x1, other arithmetic: none -> 22.1 us  [per_device(): back_hidden = (back_float * gated).astype(jnp.bfloat16)]
    unnamed x17 -> x14, local copies, waits for them, and re-layouts: 49 us -> 30.6 us
    convert_element_type x0 -> x1, local copies, waits for them, and re-layouts: none -> 11.8 us  [per_device(): back_float = back_rows.astype(jnp.float32)]
  transfers between devices with their start and end apart: 5 -> 5, of which waited for: 3 -> 4; matrix products, arithmetic and copies ran while one was open for 16% -> 21% of each run, Pallas kernels for 0% -> 0%
where the time goes in v2:
time: 899 us; the launch traced here: 897 us
  waiting for transfers between devices  508 us (57%)
  starting transfers between devices  146 us (16%)
  matrix products  117 us (13%)
  local copies, waits for them, and re-layouts  86.6 us (10%)
  other arithmetic  25.8 us (3%)
  between operations  14.1 us (2%)
    all_to_all x1, waiting for transfers between devices, per_device(): lax.all_to_all(back_send, 'seq', split_axis=0, concat_axis=0, tiled=True)  224 us
    all_to_all x1, waiting for transfers between devices, per_device(): lax.all_to_all(mixed_send, 'seq', split_axis=0, concat_axis=0, tiled=True)  198 us
    all_to_all x1, starting transfers between devices, per_device(): lax.all_to_all(mixed_send, 'seq', split_axis=0, concat_axis=0, tiled=True)  70.2 us
    all_to_all x1, starting transfers between devices, per_device(): lax.all_to_all(part_second.reshape(shards, shard_rows, extent), 'seq', sp...  70.2 us
    reduce_scatter x1, waiting for transfers between devices, per_device(): lax.psum_scatter(part_first, 'seq', scatter_dimension=0, tiled=True)  62.5 us
    reshape x2, local copies, waits for them, and re-layouts, per_device(): mixed_send = mixed.reshape(rows, shards, cols * channels).transpose(1, 0, 2)  44.2 us
    dot_general x1, matrix products, per_device(): jnp.einsum('ikc,kj->ijc', back_hidden, full_first, preferred_element_type...  34.4 us
    unnamed x14, local copies, waits for them, and re-layouts  30.6 us
  transfers between devices with their start and end apart: 5, of which 4 were waited for; matrix products, arithmetic and copies ran while one was open for 21% of the time, Pallas kernels for 0%

profile of v2, /device:TPU:0, one launch (start us, length us, event | category | flops | bytes accessed | tf_op | source)
XLA Modules:
  0.0 897.1 jit_solution(13065297065728940712)
XLA Ops:
  7.2 0.0 all-gather.2.cloned.1.call-start
  7.2 1.0 fusion.4
  8.2 0.0 copy-start.1
  8.2 1.0 fusion.7
  9.2 0.0 copy-start.3
  9.2 0.8 fusion.13
  10.0 0.6 pad_maximum_fusion
  10.7 0.0 all-gather.2.cloned.1.call-update
  10.7 18.4 %copy.17 = bf16[64,8,32,512]{3,1,2,0:T(8,128)(2,1)} copy(bf16[64,8,32,512]{3,2,1,0:T(8,128)(2,1)} %bitcast.65) | data formatting | bytes 33554432
  29.1 0.0 copy-done.1
  29.1 0.0 copy-done.3
  29.1 22.4 %all-gather.2.cloned.1.call-done = bf16[2,512,512]{2,1,0:T(8,128)(2,1)} async-done(((bf16[2,32,512]{2,1,0:T(8,128)(2,1)}), bf16[2,512,512]{2,1,0:T(8,128)(2,1)}) %all-gather.2.cloned.1.call-update) | async-done | bytes 1048592 | tf_op jit(solution)/shard_map/all_gather | solution.py:30
  51.5 16.0 %convolution_convert_fusion = bf16[512,16384]{1,0:T(8,128)(2,1)} fusion(bf16[512,16384]{1,0:T(8,128)(2,1)} %bitcast.61, bf16[2,512,512]{2,1,0:T(8,128)(2,1)} %all-gather.2.cloned.1.call-done), kind=kOutput, calls=%fused_computation.9 | convolution fusion | flops 8598323200 | bytes 34078720 | tf_op jit(solution)/shard_map/dot_general | solution.py:36
  67.5 0.0 copy-start.5
  67.5 0.0 copy-start
  67.5 5.3 all-to-all-start
  72.8 0.0 copy-done.5
  72.8 0.0 copy-done
  72.8 28.2 %fusion.3 = (bf16[32,512,512]{2,1,0:T(8,128)(2,1)}, f32[512,32,512]{2,0,1:T(8,128)}) fusion(bf16[32,512,512]{2,1,0:T(8,128)(2,1)} %param.7, f32[32,512]{1,0:T(8,128)S(1)} %convert_element_type.60, bf16[2,512,512]{2,1,0:T(8,128)(2,1)S(1)} %copy-done), kind=kOutput, calls=%fused_computation.7 | convolution fusion | flops 8623489024 | bytes 84475904 | tf_op jit(solution)/shard_map/ijc,kj->ikc/dot_general | solution.py:44
  101.0 25.6 %reshape.62 = bf16[32,16,16384]{2,1,0:T(8,128)(2,1)} reshape(bf16[32,512,512]{2,1,0:T(8,128)(2,1)} %get-tuple-element.13) | data formatting | bytes 33554432 | tf_op jit(solution)/shard_map/reshape | solution.py:46
  126.7 18.5 %copy.20 = bf16[32,16,16384]{2,0,1:T(8,128)(2,1)} copy(bf16[32,16,16384]{2,1,0:T(8,128)(2,1)} %reshape.62) | data formatting | bytes 33554432 | tf_op jit(solution)/shard_map/reshape | solution.py:46
  145.2 224.3 %all-to-all-done = bf16[16,32,16384]{2,1,0:T(8,128)(2,1)} async-done(((bf16[16,32,16384]{2,1,0:T(8,128)(2,1)}), bf16[16,32,16384]{2,1,0:T(8,128)(2,1)}, u32[]{:S(2)}, u32[]{:S(2)}) %all-to-all-start) | async-done | bytes 16777248 | tf_op jit(solution)/shard_map/all_to_all | solution.py:40
  369.5 70.2 %all-to-all-start.1 = ((bf16[16,32,16384]{2,1,0:T(8,128)(2,1)}), bf16[16,32,16384]{2,1,0:T(8,128)(2,1)}, u32[]{:S(2)}, u32[]{:S(2)}) async-start(bf16[16,32,16384]{2,1,0:T(8,128)(2,1)} %bitcast.64), calls=%async_computation.1 | async-start | bytes 33554432 | tf_op jit(solution)/shard_map/all_to_all | solution.py:48
  439.7 12.1 %copy.18 = f32[64,8,32,512]{3,2,1,0:T(8,128)S(1)} copy(bf16[64,8,32,512]{3,1,2,0:T(8,128)(2,1)} %bitcast.49) | data formatting | bytes 50331648
  451.9 11.8 %copy.13 = f32[16,32,32,512]{3,2,0,1:T(8,128)} copy(f32[16,32,32,512]{3,2,1,0:T(8,128)S(1)} %bitcast.60) | data formatting | bytes 67108864 | tf_op jit(solution)/shard_map/convert_element_type | solution.py:52
  463.7 22.1 %fusion.2 = bf16[32,512,512]{2,1,0:T(8,128)(2,1)} fusion(f32[16,32,32,512]{3,2,0,1:T(8,128)} %copy.13, bf16[32,512,512]{2,1,0:T(8,128)(2,1)} %param.7, f32[32,512]{1,0:T(8,128)S(1)} %convert_element_type.60), kind=kLoop, calls=%fused_computation.5 | loop fusion | flops 33554432 | bytes 67174400 | tf_op jit(solution)/shard_map/convert_element_type | solution.py:53
  485.8 18.0 %convolution_bitcast_fusion = f32[512,512]{1,0:T(8,128)} fusion(bf16[32,512,512]{2,1,0:T(8,128)(2,1)} %fusion.2, bf16[32,512,512]{2,1,0:T(8,128)(2,1)} %param.7), kind=kOutput, calls=%fused_computation.11 | convolution fusion | flops 8589934592 | bytes 34603008 | tf_op jit(solution)/shard_map/ikc,ijc->kj/dot_general | solution.py:57
  503.8 34.4 %fusion = bf16[32,512,512]{2,1,0:T(8,128)(2,1)} fusion(f32[16,32,32,512]{3,2,0,1:T(8,128)} %copy.13, f32[512,32,512]{2,0,1:T(8,128)} %get-tuple-element.14, f32[32,512]{1,0:T(8,128)S(1)} %convert_element_type.60, bf16[32,512,512]{2,1,0:T(8,128)(2,1)} %fusion.2, bf16[2,512,512]{2,1,0:T(8,128)(2,1)S(1)} %copy-done), kind=kOutput, calls=%fused_computation.1 | convolution fusion | flops 8623489024 | bytes 101253120 | tf_op jit(solution)/shard_map/ikc,kj->ijc/dot_general | solution.py:55
  538.2 198.3 %all-to-all-done.1 = bf16[16,32,16384]{2,1,0:T(8,128)(2,1)} async-done(((bf16[16,32,16384]{2,1,0:T(8,128)(2,1)}), bf16[16,32,16384]{2,1,0:T(8,128)(2,1)}, u32[]{:S(2)}, u32[]{:S(2)}) %all-to-all-start.1) | async-done | bytes 16777248 | tf_op jit(solution)/shard_map/all_to_all | solution.py:48
  736.5 0.0 copy-start.4
  736.5 0.0 copy-start.2
  736.5 18.1 %fusion.26 = f32[512,512]{0,1:T(8,128)} fusion(bf16[512,16384]{1,0:T(8,128)(2,1)} %bitcast.14, bf16[512,16384]{1,0:T(8,128)(2,1)} %bitcast.62), kind=kOutput, calls=%fused_computation.45 | convolution fusion | flops 8589934592 | bytes 34603008 | tf_op jit(solution)/shard_map/dot_general | solution.py:64
  754.6 70.2 %all-to-all-start.2 = ((f32[16,32,512]{2,1,0:T(8,128)}), f32[16,32,512]{2,1,0:T(8,128)S(1)}, u32[]{:S(2)}, u32[]{:S(2)}) async-start(f32[16,32,512]{2,1,0:T(8,128)} %bitcast.16), calls=%async_computation.3 | async-start | bytes 2097152 | tf_op jit(solution)/shard_map/all_to_all | solution.py:70
  824.8 0.0 reduce-scatter.2.cloned.1.call-start
  824.8 0.7 reduce-scatter.2.cloned.1.call-update
  825.5 62.5 %reduce-scatter.2.cloned.1.call-done = f32[32,512]{1,0:T(8,128)} async-done(((f32[512,512]{1,0:T(8,128)}), f32[32,512]{1,0:T(8,128)}) %reduce-scatter.2.cloned.1.call-update) | async-done | bytes 65552 | tf_op jit(solution)/shard_map/reduce_scatter | solution.py:60
  888.0 0.0 copy-done.4
  888.0 1.5 multiply_multiply_fusion.1
  889.5 0.0 all-to-all-done.2
  889.5 0.1 reduce_sum.9
  889.6 0.0 copy-done.2
  889.6 0.6 multiply_multiply_fusion
  (3 shorter events, 0.0 us)
Async XLA Ops:
  7.2 44.4 %all-gather.2.cloned.1.call-start = ((), (), s32[]{:S(2)}) async-start(), calls=%async_computation.4 | async-start | bytes 1114112 | tf_op jit(solution)/shard_map/all_gather | solution.py:30
  8.2 20.9 %copy-start.1 = (f32[32,512]{1,0:T(8,128)}, f32[32,512]{1,0:T(8,128)S(1)}, u32[]{:S(2)}) copy-start(f32[32,512]{1,0:T(8,128)S(1)} %fusion.4) | copy-start | bytes 196612
  9.2 19.9 %copy-start.3 = (f32[32,512]{1,0:T(8,128)}, f32[32,512]{1,0:T(8,128)S(1)}, u32[]{:S(2)}) copy-start(f32[32,512]{1,0:T(8,128)S(1)} %fusion.7) | copy-start | bytes 196612
  67.5 5.3 copy-start.5
  67.5 5.3 copy-start
  67.5 302.0 %all-to-all-start = ((bf16[16,32,16384]{2,1,0:T(8,128)(2,1)}), bf16[16,32,16384]{2,1,0:T(8,128)(2,1)}, u32[]{:S(2)}, u32[]{:S(2)}) async-start(bf16[16,32,16384]{2,1,0:T(8,128)(2,1)} %bitcast.63), calls=%async_computation | async-start | bytes 33554432 | tf_op jit(solution)/shard_map/all_to_all | solution.py:40
  369.5 367.0 %all-to-all-start.1 = ((bf16[16,32,16384]{2,1,0:T(8,128)(2,1)}), bf16[16,32,16384]{2,1,0:T(8,128)(2,1)}, u32[]{:S(2)}, u32[]{:S(2)}) async-start(bf16[16,32,16384]{2,1,0:T(8,128)(2,1)} %bitcast.64), calls=%async_computation.1 | async-start | bytes 33554432 | tf_op jit(solution)/shard_map/all_to_all | solution.py:48
  736.5 151.5 %copy-start.4 = (f32[32,512]{1,0:T(8,128)S(1)}, f32[32,512]{1,0:T(8,128)}, u32[]{:S(2)}) copy-start(f32[32,512]{1,0:T(8,128)} %copy-done.3) | copy-start | bytes 196612
  736.5 153.1 %copy-start.2 = (f32[32,512]{1,0:T(8,128)S(1)}, f32[32,512]{1,0:T(8,128)}, u32[]{:S(2)}) copy-start(f32[32,512]{1,0:T(8,128)} %copy-done.1) | copy-start | bytes 196612
  754.6 134.9 %all-to-all-start.2 = ((f32[16,32,512]{2,1,0:T(8,128)}), f32[16,32,512]{2,1,0:T(8,128)S(1)}, u32[]{:S(2)}, u32[]{:S(2)}) async-start(f32[16,32,512]{2,1,0:T(8,128)} %bitcast.16), calls=%async_computation.3 | async-start | bytes 2097152 | tf_op jit(solution)/shard_map/all_to_all | solution.py:70
  824.8 63.2 %reduce-scatter.2.cloned.1.call-start = ((), (), s32[]{:S(2)}) async-start(), calls=%async_computation.5 | async-start | bytes 1114112 | tf_op jit(solution)/shard_map/reduce_scatter | solution.py:60
Sparse Core Ops, SparseCore 0:
  10.8 40.6 all-gather.1
  829.3 58.7 reduce-scatter.1

commit v3 on v2

--- a/solution.py
+++ b/solution.py
@@ -58,8 +58,8 @@
         "ikc,ijc->kj", back_hidden, tokens_late, preferred_element_type=jnp.float32
     )
     summed_first = lax.psum_scatter(part_first, "seq", scatter_dimension=0, tiled=True)
-    flat_cols, grad_tokens, part_first = lax.optimization_barrier(
-        (flat_cols, grad_tokens, part_first)
+    flat_cols, grad_tokens, summed_first = lax.optimization_barrier(
+        (flat_cols, grad_tokens, summed_first)
     )
     part_second = lax.dot_general(
         flat_cot,

time: 899 us -> 864 us (0.961)
  waiting for transfers between devices: 508 us -> 473 us
    all_to_all x1, waiting for transfers between devices: 198 us -> 20.6 us  [per_device(): lax.all_to_all(mixed_send, 'seq', split_axis=0, concat_axis=0, tiled=True)]
    reduce_scatter x1, waiting for transfers between devices: 62.5 us -> 183 us  [per_device(): lax.psum_scatter(part_first, 'seq', scatter_dimension=0, tiled=True)]
    all_to_all x1, waiting for transfers between devices: 0.01 us -> 22.3 us  [per_device(): lax.all_to_all(part_second.reshape(shards, shard_rows, extent), 'seq', sp...]
    unnamed x14 -> x16, local copies, waits for them, and re-layouts: 30.6 us -> 30.6 us
  transfers between devices with their start and end apart: 5 -> 5, of which waited for: 4 -> 5; matrix products, arithmetic and copies ran while one was open for 21% -> 22% of each run, Pallas kernels for 0% -> 0%
where the time goes in v3:
time: 864 us; the launch traced here: 862 us
  waiting for transfers between devices  473 us (55%)
  starting transfers between devices  146 us (17%)
  matrix products  117 us (14%)
  local copies, waits for them, and re-layouts  86.6 us (10%)
  other arithmetic  24.9 us (3%)
  between operations  14.2 us (2%)
    all_to_all x1, waiting for transfers between devices, per_device(): lax.all_to_all(back_send, 'seq', split_axis=0, concat_axis=0, tiled=True)  224 us
    reduce_scatter x1, waiting for transfers between devices, per_device(): lax.psum_scatter(part_first, 'seq', scatter_dimension=0, tiled=True)  183 us
    all_to_all x1, starting transfers between devices, per_device(): lax.all_to_all(mixed_send, 'seq', split_axis=0, concat_axis=0, tiled=True)  70.2 us
    all_to_all x1, starting transfers between devices, per_device(): lax.all_to_all(part_second.reshape(shards, shard_rows, extent), 'seq', sp...  70.2 us
    reshape x2, local copies, waits for them, and re-layouts, per_device(): mixed_send = mixed.reshape(rows, shards, cols * channels).transpose(1, 0, 2)  44.1 us
    dot_general x1, matrix products, per_device(): jnp.einsum('ikc,kj->ijc', back_hidden, full_first, preferred_element_type...  35 us
    unnamed x16, local copies, waits for them, and re-layouts  30.6 us
    dot_general x1, matrix products, per_device(): jnp.einsum('ijc,kj->ikc', tokens_late, full_first, preferred_element_type...  28.2 us
  transfers between devices with their start and end apart: 5, of which 5 were waited for; matrix products, arithmetic and copies ran while one was open for 22% of the time, Pallas kernels for 0%

profile of v3, /device:TPU:0, one launch (start us, length us, event | category | flops | bytes accessed | tf_op | source)
XLA Modules:
  0.0 861.6 jit_solution(17348475536312043015)
XLA Ops:
  7.2 0.0 all-gather.2.cloned.1.call-start
  7.2 1.0 fusion.4
  8.2 0.0 copy-start.1
  8.2 1.0 fusion.7
  9.2 0.0 copy-start.3
  9.2 0.8 fusion.13
  10.0 0.6 pad_maximum_fusion
  10.7 0.0 all-gather.2.cloned.1.call-update
  10.7 18.4 %copy.17 = bf16[64,8,32,512]{3,1,2,0:T(8,128)(2,1)} copy(bf16[64,8,32,512]{3,2,1,0:T(8,128)(2,1)} %bitcast.65) | data formatting | bytes 33554432
  29.1 0.0 copy-done.1
  29.1 0.0 copy-done.3
  29.1 22.4 %all-gather.2.cloned.1.call-done = bf16[2,512,512]{2,1,0:T(8,128)(2,1)} async-done(((bf16[2,32,512]{2,1,0:T(8,128)(2,1)}), bf16[2,512,512]{2,1,0:T(8,128)(2,1)}) %all-gather.2.cloned.1.call-update) | async-done | bytes 1048592 | tf_op jit(solution)/shard_map/all_gather | solution.py:30
  51.5 16.0 %convolution_convert_fusion = bf16[512,16384]{1,0:T(8,128)(2,1)} fusion(bf16[512,16384]{1,0:T(8,128)(2,1)} %bitcast.61, bf16[2,512,512]{2,1,0:T(8,128)(2,1)} %all-gather.2.cloned.1.call-done), kind=kOutput, calls=%fused_computation.9 | convolution fusion | flops 8598323200 | bytes 34078720 | tf_op jit(solution)/shard_map/dot_general | solution.py:36
  67.5 0.0 copy-start.6
  67.5 0.0 copy-start
  67.5 5.3 all-to-all-start
  72.8 0.0 copy-done.6
  72.8 0.0 copy-done
  72.8 28.2 %fusion.3 = (bf16[32,512,512]{2,1,0:T(8,128)(2,1)}, f32[512,32,512]{2,0,1:T(8,128)}) fusion(bf16[32,512,512]{2,1,0:T(8,128)(2,1)} %param.7, f32[32,512]{1,0:T(8,128)S(1)} %convert_element_type.60, bf16[2,512,512]{2,1,0:T(8,128)(2,1)S(1)} %copy-done), kind=kOutput, calls=%fused_computation.7 | convolution fusion | flops 8623489024 | bytes 84475904 | tf_op jit(solution)/shard_map/ijc,kj->ikc/dot_general | solution.py:44
  101.0 25.6 %reshape.62 = bf16[32,16,16384]{2,1,0:T(8,128)(2,1)} reshape(bf16[32,512,512]{2,1,0:T(8,128)(2,1)} %get-tuple-element.15) | data formatting | bytes 33554432 | tf_op jit(solution)/shard_map/reshape | solution.py:46
  126.7 18.5 %copy.20 = bf16[32,16,16384]{2,0,1:T(8,128)(2,1)} copy(bf16[32,16,16384]{2,1,0:T(8,128)(2,1)} %reshape.62) | data formatting | bytes 33554432 | tf_op jit(solution)/shard_map/reshape | solution.py:46
  145.2 224.3 %all-to-all-done = bf16[16,32,16384]{2,1,0:T(8,128)(2,1)} async-done(((bf16[16,32,16384]{2,1,0:T(8,128)(2,1)}), bf16[16,32,16384]{2,1,0:T(8,128)(2,1)}, u32[]{:S(2)}, u32[]{:S(2)}) %all-to-all-start) | async-done | bytes 16777248 | tf_op jit(solution)/shard_map/all_to_all | solution.py:40
  369.5 70.2 %all-to-all-start.1 = ((bf16[16,32,16384]{2,1,0:T(8,128)(2,1)}), bf16[16,32,16384]{2,1,0:T(8,128)(2,1)}, u32[]{:S(2)}, u32[]{:S(2)}) async-start(bf16[16,32,16384]{2,1,0:T(8,128)(2,1)} %bitcast.64), calls=%async_computation.1 | async-start | bytes 33554432 | tf_op jit(solution)/shard_map/all_to_all | solution.py:48
  439.7 0.2 reduce-scatter.2.cloned.1.call-start
  440.0 12.1 %copy.18 = f32[64,8,32,512]{3,2,1,0:T(8,128)S(1)} copy(bf16[64,8,32,512]{3,1,2,0:T(8,128)(2,1)} %bitcast.49) | data formatting | bytes 50331648
  452.1 11.9 %copy.13 = f32[16,32,32,512]{3,2,0,1:T(8,128)} copy(f32[16,32,32,512]{3,2,1,0:T(8,128)S(1)} %bitcast.60) | data formatting | bytes 67108864 | tf_op jit(solution)/shard_map/convert_element_type | solution.py:52
  463.9 22.1 %fusion.2 = bf16[32,512,512]{2,1,0:T(8,128)(2,1)} fusion(f32[16,32,32,512]{3,2,0,1:T(8,128)} %copy.13, bf16[32,512,512]{2,1,0:T(8,128)(2,1)} %param.7, f32[32,512]{1,0:T(8,128)S(1)} %convert_element_type.60), kind=kLoop, calls=%fused_computation.5 | loop fusion | flops 33554432 | bytes 67174400 | tf_op jit(solution)/shard_map/convert_element_type | solution.py:53
  486.0 18.0 %convolution_bitcast_fusion = f32[512,512]{1,0:T(8,128)} fusion(bf16[32,512,512]{2,1,0:T(8,128)(2,1)} %fusion.2, bf16[32,512,512]{2,1,0:T(8,128)(2,1)} %param.7), kind=kOutput, calls=%fused_computation.11 | convolution fusion | flops 8589934592 | bytes 34603008 | tf_op jit(solution)/shard_map/ikc,ijc->kj/dot_general | solution.py:57
  504.1 0.0 reduce-scatter.2.cloned.1.call-update
  504.1 35.0 %fusion = bf16[32,512,512]{2,1,0:T(8,128)(2,1)} fusion(f32[16,32,32,512]{3,2,0,1:T(8,128)} %copy.13, f32[512,32,512]{2,0,1:T(8,128)} %get-tuple-element.16, f32[32,512]{1,0:T(8,128)S(1)} %convert_element_type.60, bf16[32,512,512]{2,1,0:T(8,128)(2,1)} %fusion.2, bf16[2,512,512]{2,1,0:T(8,128)(2,1)S(1)} %copy-done), kind=kOutput, calls=%fused_computation.1 | convolution fusion | flops 8623489024 | bytes 101253120 | tf_op jit(solution)/shard_map/ikc,kj->ijc/dot_general | solution.py:55
  539.1 183.1 %reduce-scatter.2.cloned.1.call-done = f32[32,512]{1,0:T(8,128)} async-done(((f32[512,512]{1,0:T(8,128)}), f32[32,512]{1,0:T(8,128)}) %reduce-scatter.2.cloned.1.call-update) | async-done | bytes 65552 | tf_op jit(solution)/shard_map/reduce_scatter | solution.py:60
  722.2 20.6 %all-to-all-done.1 = bf16[16,32,16384]{2,1,0:T(8,128)(2,1)} async-done(((bf16[16,32,16384]{2,1,0:T(8,128)(2,1)}), bf16[16,32,16384]{2,1,0:T(8,128)(2,1)}, u32[]{:S(2)}, u32[]{:S(2)}) %all-to-all-start.1) | async-done | bytes 16777248 | tf_op jit(solution)/shard_map/all_to_all | solution.py:48
  742.8 0.0 copy-start.4
  742.8 0.0 copy-start.5
  742.8 0.0 copy-start.2
  742.8 18.1 %fusion.26 = f32[512,512]{0,1:T(8,128)} fusion(bf16[512,16384]{1,0:T(8,128)(2,1)} %bitcast.14, bf16[512,16384]{1,0:T(8,128)(2,1)} %bitcast.62), kind=kOutput, calls=%fused_computation.45 | convolution fusion | flops 8589934592 | bytes 34603008 | tf_op jit(solution)/shard_map/dot_general | solution.py:64
  760.9 70.2 %all-to-all-start.2 = ((f32[16,32,512]{2,1,0:T(8,128)}), f32[16,32,512]{2,1,0:T(8,128)S(1)}, u32[]{:S(2)}, u32[]{:S(2)}) async-start(f32[16,32,512]{2,1,0:T(8,128)} %bitcast.16), calls=%async_computation.3 | async-start | bytes 2097152 | tf_op jit(solution)/shard_map/all_to_all | solution.py:70
  831.1 0.0 copy-done.4
  831.1 0.0 copy-done.5
  831.1 0.6 multiply_multiply_fusion.1
  831.8 22.3 %all-to-all-done.2 = f32[16,32,512]{2,1,0:T(8,128)S(1)} async-done(((f32[16,32,512]{2,1,0:T(8,128)}), f32[16,32,512]{2,1,0:T(8,128)S(1)}, u32[]{:S(2)}, u32[]{:S(2)}) %all-to-all-start.2) | async-done | bytes 1048608 | tf_op jit(solution)/shard_map/all_to_all | solution.py:70
  854.0 0.1 reduce_sum.9
  854.1 0.0 copy-done.2
  854.1 0.6 multiply_multiply_fusion
  (3 shorter events, 0.0 us)
Async XLA Ops:
  7.2 44.4 %all-gather.2.cloned.1.call-start = ((), (), s32[]{:S(2)}) async-start(), calls=%async_computation.4 | async-start | bytes 1114112 | tf_op jit(solution)/shard_map/all_gather | solution.py:30
  8.2 20.9 %copy-start.1 = (f32[32,512]{1,0:T(8,128)}, f32[32,512]{1,0:T(8,128)S(1)}, u32[]{:S(2)}) copy-start(f32[32,512]{1,0:T(8,128)S(1)} %fusion.4) | copy-start | bytes 196612
  9.2 19.9 %copy-start.3 = (f32[32,512]{1,0:T(8,128)}, f32[32,512]{1,0:T(8,128)S(1)}, u32[]{:S(2)}) copy-start(f32[32,512]{1,0:T(8,128)S(1)} %fusion.7) | copy-start | bytes 196612
  67.5 5.3 copy-start.6
  67.5 5.3 copy-start
  67.5 302.0 %all-to-all-start = ((bf16[16,32,16384]{2,1,0:T(8,128)(2,1)}), bf16[16,32,16384]{2,1,0:T(8,128)(2,1)}, u32[]{:S(2)}, u32[]{:S(2)}) async-start(bf16[16,32,16384]{2,1,0:T(8,128)(2,1)} %bitcast.63), calls=%async_computation | async-start | bytes 33554432 | tf_op jit(solution)/shard_map/all_to_all | solution.py:40
  369.5 373.3 %all-to-all-start.1 = ((bf16[16,32,16384]{2,1,0:T(8,128)(2,1)}), bf16[16,32,16384]{2,1,0:T(8,128)(2,1)}, u32[]{:S(2)}, u32[]{:S(2)}) async-start(bf16[16,32,16384]{2,1,0:T(8,128)(2,1)} %bitcast.64), calls=%async_computation.1 | async-start | bytes 33554432 | tf_op jit(solution)/shard_map/all_to_all | solution.py:48
  439.7 282.5 %reduce-scatter.2.cloned.1.call-start = ((), (), s32[]{:S(2)}) async-start(), calls=%async_computation.5 | async-start | bytes 1114112 | tf_op jit(solution)/shard_map/reduce_scatter | solution.py:60
  742.8 88.3 %copy-start.4 = (f32[32,512]{1,0:T(8,128)S(1)}, f32[32,512]{1,0:T(8,128)}, u32[]{:S(2)}) copy-start(f32[32,512]{1,0:T(8,128)} %copy-done.3) | copy-start | bytes 196612
  742.8 88.3 %copy-start.5 = (f32[32,512]{1,0:T(8,128)S(1)}, f32[32,512]{1,0:T(8,128)}, u32[]{:S(2)}) copy-start(f32[32,512]{1,0:T(8,128)} %reduce-scatter.2.cloned.1.call-done) | copy-start | bytes 196612
  742.8 111.3 %copy-start.2 = (f32[32,512]{1,0:T(8,128)S(1)}, f32[32,512]{1,0:T(8,128)}, u32[]{:S(2)}) copy-start(f32[32,512]{1,0:T(8,128)} %copy-done.1) | copy-start | bytes 196612
  760.9 93.1 %all-to-all-start.2 = ((f32[16,32,512]{2,1,0:T(8,128)}), f32[16,32,512]{2,1,0:T(8,128)S(1)}, u32[]{:S(2)}, u32[]{:S(2)}) async-start(f32[16,32,512]{2,1,0:T(8,128)} %bitcast.16), calls=%async_computation.3 | async-start | bytes 2097152 | tf_op jit(solution)/shard_map/all_to_all | solution.py:70
Sparse Core Ops, SparseCore 0:
  10.8 40.6 all-gather.1
  504.2 217.9 reduce-scatter.1
